TPU v7x, 32 devices: a whole 2x2x4 slice. The times are simulated.
32 devices in a mesh: obs: 8 (over z, y), coef: 4 (over x, core).
Axes of the slice: x: 2, y: 2, z: 4, core: 2. Of those that a mesh axis runs over, the one named last changes fastest.
Arguments:
- design: bfloat16 [8192, 36864], P('obs', 'coef'), may hold values from -0.03125 to 0.03125
- observations: bfloat16 [8, 8192], P(None, 'obs'), may hold values from -6 to 6
- shift_table: float32 [16], replicated, may hold values from 0.1 to 3
- shift_index: int32 [8], replicated, may hold values from 0 to 15
- coef_perm: int32 [36864], P('coef'), may hold values from 0 to 36863, as said below
- order_map: int32 [8], replicated, may hold values from 0 to 7, each once
Outputs:
- band_fourier: float32 [192, 2, 8, 32], P('coef', None, None, 'obs')
- field: float32 [8, 32, 1024], P(None, ('obs', 'coef'))
Inputs may be any that keep to these rules, and one draw needn't show every extreme that they name: coef_perm is a permutation; the design columns of each block of 9216 consecutive columns hold exactly 1152 values of each range of 4608 consecutive values. `order_map`: each block number appears once.
All inputs are finite; a program needn't handle non-finite values.
Results may differ from a plain program's by a relative error of at most 0.007.
Values may be sent and summed in bfloat16 or wider, within the bound.
A program may use at most 64 MiB of HBM per device.

v0:
```python
import math

import jax
import jax.numpy as jnp
from jax import lax
from jax.sharding import PartitionSpec as P

NL = 192
COLS = 8
ITERS = 2
NSHIFT = 16
BPO = 2
NLON = 1024
LAT_DEV = 1


CENTRE_OFFSET = 1.25
HALF_WIDTH = 0.95


def legendre_table(orders, colatitude, degrees):
    cosine = jnp.cos(colatitude)
    sine = jnp.sin(colatitude)
    order_value = orders.astype(sine.dtype)[:, None]

    def advance(carry, degree):
        diagonal, previous, earlier = carry
        level = degree.astype(sine.dtype)
        safe_level = jnp.maximum(level, 1.0)
        grown = diagonal * sine * jnp.sqrt((2.0 * safe_level + 1.0) / (2.0 * safe_level))
        diagonal_next = jnp.where(
            degree == 0, jnp.ones_like(sine), jnp.where(degree == 1, jnp.sqrt(3.0) * sine, grown)
        )
        above = level > order_value
        product = (level - order_value) * (level + order_value)
        denom = jnp.where(above, product, 1.0)
        first = jnp.sqrt(jnp.maximum((2.0 * level - 1.0) * (2.0 * level + 1.0), 0.0) / denom)
        second = jnp.sqrt(
            jnp.maximum(
                (2.0 * level + 1.0) * (level + order_value - 1.0) * (level - order_value - 1.0), 0.0
            )
            / (denom * jnp.maximum(2.0 * level - 3.0, 1.0))
        )
        recur = first * cosine[None, :] * previous - second * earlier
        value = jnp.where(
            above, recur, jnp.where(level == order_value, diagonal_next[None, :], 0.0)
        )
        return ((diagonal_next, value, previous), value)

    start = jnp.zeros((orders.shape[0], colatitude.shape[0]), sine.dtype)
    final_state, table = lax.scan(
        advance,
        (jnp.zeros_like(sine), start, start),
        jnp.arange(degrees, dtype=jnp.int32),
        unroll=16,
    )
    return table


def wave_tables(rows, longitudes):
    steps_k = jnp.arange(longitudes, dtype=jnp.int32)
    scale = 2.0 * math.pi / longitudes
    cos_angle = (rows[:, None] * steps_k[None, :] % longitudes).astype(jnp.float32) * scale
    sin_angle = ((NL - rows)[:, None] * steps_k[None, :] % longitudes).astype(jnp.float32) * scale
    return (jnp.cos(cos_angle), jnp.sin(sin_angle))


def body(design, observations, shift_table, shift_index, coef_perm, order_map):
    obs_count = lax.axis_size("obs")
    coef_count = lax.axis_size("coef")
    coef_rank = lax.axis_index("coef")
    obs_rank = lax.axis_index("obs")
    kdev = design.shape[1]
    table_index = jnp.arange(NSHIFT, dtype=jnp.int32)
    shifts = jnp.sum(
        jnp.where(shift_index[:, None] == table_index[None, :], shift_table[None, :], 0.0), axis=1
    )
    centre = shifts + CENTRE_OFFSET
    ratio_start = centre / HALF_WIDTH

    def reduce_normal(partial_normal):
        return lax.psum(partial_normal, "obs")

    residual = reduce_normal(jnp.dot(observations, design, preferred_element_type=jnp.float32))
    solution = jnp.zeros_like(residual)
    factor = 1.0 / ratio_start
    direction = residual / centre[:, None]
    for iteration in range(ITERS):
        solution = solution + direction
        partial_image = lax.dot_general(
            direction.astype(jnp.bfloat16),
            design,
            (((1,), (1,)), ((), ())),
            preferred_element_type=jnp.float32,
        )
        image = lax.psum(partial_image, "coef")
        normal = reduce_normal(
            jnp.dot(image.astype(jnp.bfloat16), design, preferred_element_type=jnp.float32)
        )
        residual = residual - (normal + shifts[:, None] * direction)
        factor_next = 1.0 / (2.0 * ratio_start - factor)
        direction = (factor_next * factor)[:, None] * direction + (2.0 * factor_next / HALF_WIDTH)[
            :, None
        ] * residual
        factor = factor_next
    solution = solution + direction
    block_count = coef_count * BPO
    block_rows = NL // block_count
    block_ids = jnp.arange(block_count, dtype=jnp.int32)
    position = jnp.sum(
        jnp.where(order_map[:, None] == block_ids[None, :], block_ids[:, None], 0), axis=0
    )

    def lookup(blocks):
        return jnp.sum(
            jnp.where(blocks[:, None] == block_ids[None, :], position[None, :], 0), axis=1
        )

    owner = lookup(coef_perm // (block_rows * NL)) // BPO
    owners = jnp.arange(coef_count, dtype=jnp.int32)
    marks = (owner[:, None] == owners[None, :]).astype(jnp.int32)
    rank = jnp.sum((jnp.cumsum(marks, axis=0) - marks) * marks, axis=1)
    per_owner = kdev // coef_count
    slot = owner * per_owner + rank
    outgoing = (
        jnp.zeros_like(solution).at[:, slot].set(solution).reshape(COLS, coef_count, per_owner)
    )
    labels = (
        jnp.zeros((kdev,), jnp.float32)
        .at[slot]
        .set(coef_perm.astype(jnp.float32))
        .reshape(1, coef_count, per_owner)
    )
    incoming, incoming_labels = (
        lax.all_to_all(outgoing, "coef", split_axis=1, concat_axis=1, tiled=True),
        lax.all_to_all(labels, "coef", split_axis=1, concat_axis=1, tiled=True),
    )
    canonical = incoming_labels.reshape(kdev).astype(jnp.int32)
    paired_row = canonical // NL
    column = canonical % NL
    local_row = lookup(paired_row // block_rows) % BPO * block_rows + paired_row % block_rows
    owned_rows = kdev // NL
    local = (
        jnp.zeros((COLS, owned_rows * NL), jnp.float32)
        .at[:, local_row * NL + column]
        .set(incoming.reshape(COLS, kdev))
        .reshape(COLS, owned_rows, NL)
    )
    my_blocks = lax.dynamic_slice_in_dim(order_map, coef_rank * BPO, BPO)
    row_offsets = jnp.arange(block_rows, dtype=jnp.int32)
    owned_canon = (my_blocks[:, None] * block_rows + row_offsets[None, :]).reshape(owned_rows)
    lat_block = LAT_DEV * coef_count
    lat_total = lat_block * obs_count
    lat_ids = obs_rank * lat_block + jnp.arange(lat_block, dtype=jnp.int32)
    colatitude = math.pi * (lat_ids.astype(jnp.float32) + 0.5) / lat_total
    both_orders = jnp.concatenate([owned_canon, NL - owned_canon], axis=0)
    both_leg = legendre_table(both_orders, colatitude, NL)
    cos_leg = both_leg[:, :owned_rows]
    sin_leg = both_leg[:, owned_rows:]
    roll_index = (jnp.arange(NL, dtype=jnp.int32)[None, :] - owned_canon[:, None]) % NL
    shifted = jnp.take_along_axis(local, roll_index[None, :, :], axis=2)
    cos_part = jnp.einsum("dqt,cqd->qct", cos_leg, shifted, precision=lax.Precision.HIGHEST)
    sin_part = jnp.einsum("dqt,cqd->qct", sin_leg, local, precision=lax.Precision.HIGHEST)
    band = jnp.stack([cos_part, sin_part], axis=1) / math.sqrt(NL)
    own_cos, own_sin = wave_tables(owned_canon, NLON)
    first_sum = jnp.einsum("qcl,qk->lck", band[:, 0], own_cos, precision=lax.Precision.HIGHEST)
    second_sum = jnp.einsum("qcl,qk->lck", band[:, 1], own_sin, precision=lax.Precision.HIGHEST)
    field = lax.psum_scatter(
        (first_sum + second_sum) / math.sqrt(NL), "coef", scatter_dimension=0, tiled=True
    ).transpose(1, 0, 2)
    return (band, field)


def solution(mesh):
    placed = (P("obs", "coef"), P(None, "obs"), P(), P(), P("coef"), P())
    return jax.shard_map(
        body,
        mesh=mesh,
        in_specs=placed,
        out_specs=(P("coef", None, None, "obs"), P(None, ("obs", "coef"), None)),
        check_vma=False,
    )
```

profile of v0, /device:TPU:0, one launch (start us, length us, event | category | flops | bytes accessed | tf_op | source)
XLA Modules:
  0.0 899.9 jit_solution(11455287304831355050)
XLA Ops:
  7.2 0.7 select_reduce_fusion.3
  7.9 0.9 fusion.122
  9.1 1.2 reduce-window.6
  10.3 0.2 slice_reduce_fusion
  10.5 0.3 reduce-window.9
  11.2 34.8 %scatter_custom_fusion = f32[9216]{0:T(1024)} fusion(s32[9216]{0:T(1024)S(1)} %bitcast.658, f32[9216]{0:T(1024)S(1)} %get-tuple-element.449, f32[]{:T(128)} %constant.291.clone.1), kind=kCustom, calls=%fused_computation.310 | custom fusion | bytes 36868 | tf_op jit(solution)/shard_map/scatter | solution.py:131
  46.0 4.2 all-to-all-start
  50.3 9.6 %fusion.124 = f32[8,9216]{1,0:T(8,128)} fusion(bf16[8,1024]{1,0:T(8,128)(2,1)S(1)} %copy-done, bf16[1024,9216]{1,0:T(8,128)(2,1)} %param.8), kind=kOutput, calls=%fused_computation.348 | convolution fusion | flops 150994944 | bytes 19185664 | tf_op jit(solution)/shard_map/dot_general | solution.py:84
  60.8 391.3 %while.22 = (s32[]{:T(128)}, f32[4]{0:T(128)S(1)}, f32[96,4]{0,1:T(4,128)S(1)}, f32[96,4]{0,1:T(4,128)S(1)}, f32[12,16,96,4]{2,1,0,3:T(8,128)S(1)}, /*index=5*/s...) while((s32[]{:T(128)}, f32[4]{0:T(128)S(1)}, ...), condition=%wide.region_16.17_spmd.clone.clone.clone, body=%wide.region_15.16_spmd.clone.clone.clone.sunk | while | flops 63018 | bytes 263757 | solution.py:51
  60.8 0.7 fusion.142
  93.5 0.7 fusion.142
  126.1 0.7 fusion.142
  158.7 0.7 fusion.142
  191.3 0.7 fusion.142
  223.9 0.7 fusion.142
  256.5 0.7 fusion.142
  289.1 0.7 fusion.142
  321.7 0.7 fusion.142
  354.3 0.7 fusion.142
  386.9 0.7 fusion.142
  419.6 0.7 fusion.142
  453.0 9.0 fusion.66
  462.0 11.9 %psum.36 = bf16[8,1024]{1,0:T(8,128)(2,1)S(1)} all-reduce(f32[8,1024]{1,0:T(8,128)S(1)} %fusion.66), channel_id=1, replica_groups=mesh['obs'=8,'coef'=4] {'coef'}, use_global_device_ids=true, to_apply=%region_9.10 | all-reduce | flops 8192 | bytes 49152 | tf_op jit(solution)/shard_map/psum | solution.py:96
  473.9 9.7 %fusion.126 = f32[8,9216]{1,0:T(8,128)} fusion(bf16[8,1024]{1,0:T(8,128)(2,1)S(1)} %psum.36, bf16[1024,9216]{1,0:T(8,128)(2,1)} %param.8), kind=kOutput, calls=%fused_computation.350 | convolution fusion | flops 150994944 | bytes 19185664 | tf_op jit(solution)/shard_map/dot_general | solution.py:98
  484.0 0.3 and_reduce_fusion
  484.3 71.5 %all-reduce.6.cloned.1.call-done = f32[8,9216]{1,0:T(8,128)} async-done(((f32[8,9216]{1,0:T(8,128)}), f32[8,9216]{1,0:T(8,128)}) %all-reduce.6.cloned.1.call-update) | async-done | bytes 294928 | tf_op jit(solution)/shard_map/psum | solution.py:82
  555.8 9.0 fusion.60
  564.8 10.3 %psum.38 = bf16[8,1024]{1,0:T(8,128)(2,1)S(1)} all-reduce(f32[8,1024]{1,0:T(8,128)S(1)} %fusion.60), channel_id=1, replica_groups=mesh['obs'=8,'coef'=4] {'coef'}, use_global_device_ids=true, to_apply=%region_11.12 | all-reduce | flops 8192 | bytes 49152 | tf_op jit(solution)/shard_map/psum | solution.py:96
  575.1 9.7 %fusion.125 = f32[8,9216]{1,0:T(8,128)} fusion(bf16[8,1024]{1,0:T(8,128)(2,1)S(1)} %psum.38, bf16[1024,9216]{1,0:T(8,128)(2,1)} %param.8), kind=kOutput, calls=%fused_computation.349 | convolution fusion | flops 150994944 | bytes 19185664 | tf_op jit(solution)/shard_map/dot_general | solution.py:98
  585.0 70.3 %all-reduce.8.cloned.1.call-done = f32[8,9216]{1,0:T(8,128)} async-done(((f32[8,9216]{1,0:T(8,128)}), f32[8,9216]{1,0:T(8,128)}) %all-reduce.8.cloned.1.call-update) | async-done | bytes 294928 | tf_op jit(solution)/shard_map/psum | solution.py:82
  655.3 1.2 add_bitcast_fusion
  656.5 2.9 copy.49
  659.4 25.7 %scatter_custom_fusion.1 = f32[8,9216]{0,1:T(8,128)} fusion(s32[9216]{0:T(1024)S(1)} %bitcast.659, f32[9216,8]{1,0:T(8,128)} %copy.49, f32[]{:T(128)} %constant.291.clone.1), kind=kCustom, calls=%fused_computation.179 | custom fusion | bytes 295424 | tf_op jit(solution)/shard_map/scatter | solution.py:126
  685.1 3.7 copy.50
  688.8 3.5 all-to-all-start.1
  692.3 0.4 compare_select_fusion
  692.8 5.8 all-to-all-done.1
  698.6 2.9 copy.51
  701.5 25.7 %scatter_custom_fusion.2 = f32[8,9216]{0,1:T(8,128)} fusion(s32[9216]{0:T(1024)S(1)} %bitcast.660, f32[9216,8]{1,0:T(8,128)} %copy.51, f32[]{:T(128)} %constant.291.clone.1), kind=kCustom, calls=%fused_computation.177 | custom fusion | bytes 295424 | tf_op jit(solution)/shard_map/scatter | solution.py:146
  727.2 5.8 convolution_bitcast_fusion
  733.1 134.2 %gather_fusion = f32[9216,8]{1,0:T(8,128)} fusion(f32[8,48,192]{0,2,1:T(8,128)} %bitcast.645, s32[9216]{0:T(1024)S(1)} %reshape.1704), kind=kCustom, calls=%fused_computation | custom fusion | bytes 663552 | tf_op jit(solution)/shard_map/jit(take_along_axis)/gather | solution.py:161
  867.3 3.3 copy.52
  870.7 0.5 convolution_bitcast_fusion.1
  871.3 1.1 fusion.40
  872.4 1.7 fusion.31
  874.1 0.6 copy.59
  874.7 17.3 %reduce-scatter.2.cloned.1.call-done = f32[1,8,1024]{2,1,0:T(8,128)} async-done(((f32[4,8,1024]{2,1,0:T(8,128)}), f32[1,8,1024]{2,1,0:T(8,128)}) %reduce-scatter.2.cloned.1.call-update) | async-done | bytes 32784 | tf_op jit(solution)/shard_map/reduce_scatter | solution.py:168
  892.0 1.4 copy.60
  (357 shorter events, 23.2 us)
Async XLA Ops:
  7.2 43.2 %copy-start = (bf16[8,1024]{1,0:T(8,128)(2,1)S(1)}, bf16[8,1024]{1,0:T(8,128)(2,1)}, u32[]{:S(2)}) copy-start(bf16[8,1024]{1,0:T(8,128)(2,1)} %param.9) | copy-start | bytes 49156
  46.0 437.8 %all-to-all-start = ((f32[1,4,2304]{2,0,1:T(1,128)}), f32[1,4,2304]{2,0,1:T(1,128)S(1)}, u32[]{:S(2)}, u32[]{:S(2)}) async-start(f32[1,4,2304]{2,0,1:T(1,128)} %bitcast.5), calls=%async_computation | async-start | bytes 73728 | tf_op jit(solution)/shard_map/all_to_all | solution.py:136
  50.3 9.8 %copy-start.3 = (s32[8]{0:T(128)S(1)}, s32[8]{0:T(128)}, u32[]{:S(2)}) copy-start(s32[8]{0:T(128)} %param.13) | copy-start | bytes 100
  50.3 10.3 %copy-start.4 = (f32[16]{0:T(128)S(1)}, f32[16]{0:T(128)}, u32[]{:S(2)}) copy-start(f32[16]{0:T(128)} %param.10) | copy-start | bytes 196
  50.3 10.3 %copy-start.5 = (s32[8]{0:T(128)S(1)}, s32[8]{0:T(128)}, u32[]{:S(2)}) copy-start(s32[8]{0:T(128)} %param.11) | copy-start | bytes 100
  50.3 402.7 %all-reduce.4.cloned.1.call-start = ((), (), s32[]{:S(2)}) async-start(), calls=%async_computation.3 | async-start | bytes 589824 | tf_op jit(solution)/shard_map/psum | solution.py:82
  60.0 495.8 %all-reduce.6.cloned.1.call-start = ((), (), s32[]{:S(2)}) async-start(), calls=%async_computation.4 | async-start | bytes 589824 | tf_op jit(solution)/shard_map/psum | solution.py:82
  473.9 81.9 %copy-start.1 = (f32[8,9216]{1,0:T(8,128)S(1)}, f32[8,9216]{1,0:T(8,128)}, u32[]{:S(2)}) copy-start(f32[8,9216]{1,0:T(8,128)} %all-reduce.4.cloned.1.call-done) | copy-start | bytes 884740
  483.6 171.7 %all-reduce.8.cloned.1.call-start = ((), (), s32[]{:S(2)}) async-start(), calls=%async_computation.5 | async-start | bytes 589824 | tf_op jit(solution)/shard_map/psum | solution.py:82
  575.0 80.3 %copy-start.2 = (f32[8,9216]{1,0:T(8,128)S(1)}, f32[8,9216]{1,0:T(8,128)}, u32[]{:S(2)}) copy-start(f32[8,9216]{1,0:T(8,128)} %all-reduce.6.cloned.1.call-done) | copy-start | bytes 884740
  688.8 9.8 %all-to-all-start.1 = ((f32[8,4,2304]{2,0,1:T(8,128)}), f32[8,4,2304]{2,0,1:T(8,128)S(1)}, u32[]{:S(2)}, u32[]{:S(2)}) async-start(f32[8,4,2304]{2,0,1:T(8,128)} %copy.50), calls=%async_computation.1 | async-start | bytes 589824 | tf_op jit(solution)/shard_map/all_to_all | solution.py:135
  692.3 199.7 %reduce-scatter.2.cloned.1.call-start = ((), (), s32[]{:S(2)}) async-start(), calls=%async_computation.6 | async-start | bytes 163840 | tf_op jit(solution)/shard_map/reduce_scatter | solution.py:168
Sparse Core Ops, SparseCore 0:
  60.1 73.6 all-reduce.3
  483.7 72.0 all-reduce.5
  584.9 70.3 all-reduce.7
  874.2 17.7 reduce-scatter.1
where the time goes:
time: 906 us; the launch traced here: 900 us
  loops' own time  363 us (40%)
  local copies, waits for them, and re-layouts  245 us (27%)
  waiting for transfers between devices  165 us (18%)
  matrix products  56.1 us (6%)
  other arithmetic  26.6 us (3%)
  blocking collectives  22.2 us (2%)
  between operations  14 us (2%)
    another operation x1, loops' own time, legendre_table(): lax.scan(advance, (jnp.zeros_like(sine), start, start), jnp.arange(degree...  363 us
    psum x3, waiting for transfers between devices, reduce_normal(): return lax.psum(partial_normal, 'obs')  142 us
    gather x3, local copies, waits for them, and re-layouts, body(): shifted = jnp.take_along_axis(local, roll_index[None, :, :], axis=2)  138 us
    scatter x1, local copies, waits for them, and re-layouts, body(): labels = jnp.zeros((kdev,), jnp.float32).at[slot].set(coef_perm.astype(jn...  34.8 us
    scatter x1, local copies, waits for them, and re-layouts, body(): local = jnp.zeros((COLS, owned_rows * NL), jnp.float32).at[:, local_row *...  25.7 us
    scatter x1, local copies, waits for them, and re-layouts, body(): jnp.zeros_like(solution).at[:, slot].set(solution)  25.7 us
    psum x2, blocking collectives, body(): image = lax.psum(partial_image, 'coef')  22.2 us
    dot_general x2, matrix products, body(): jnp.dot(image.astype(jnp.bfloat16), design, preferred_element_type=jnp.fl...  19.4 us
  transfers between devices with their start and end apart: 6, of which 4 were waited for; matrix products, arithmetic and copies ran while one was open for 7% of the time, Pallas kernels for 0%

commit v1 on v0

v1 whole, which is shorter than its diff:
```python
import functools
import math

import jax
import jax.numpy as jnp
from jax import lax
from jax.experimental import pallas as pl
from jax.experimental.pallas import tpu as pltpu
from jax.sharding import PartitionSpec as P

NL = 192
COLS = 8
ITERS = 2
NSHIFT = 16
BPO = 2
NLON = 1024
LAT_DEV = 1

CENTRE_OFFSET = 1.25
HALF_WIDTH = 0.95
VMEM_SPEC = pl.BlockSpec(memory_space=pltpu.VMEM)
MESH = pl.DeviceIdType.MESH


def greet(axis, n, me):
    barrier = pltpu.get_barrier_semaphore()
    for step in range(1, n):
        pl.semaphore_signal(
            barrier, inc=1, device_id={axis: lax.rem(me + step, n)}, device_id_type=MESH
        )
    pl.semaphore_wait(barrier, n - 1)


def push(axis, n, me, step, src, dst, send_sem, recv_sem):
    return pltpu.make_async_remote_copy(
        src_ref=src,
        dst_ref=dst,
        send_sem=send_sem.at[step],
        recv_sem=recv_sem.at[step],
        device_id={axis: lax.rem(me + step, n)},
        device_id_type=MESH,
    )


def normal_kernel(
    n, mode, part_ref, res_ref, dir_ref, sol_ref, shift_ref, keep_ref, gain_ref,
    res_out, dir_out, sol_out, full_out,
    landed, gathered, send_a, recv_a, send_b, recv_b,
):
    me = lax.axis_index("obs")
    chunk = res_ref.shape[1]
    greet("obs", n, me)
    copies = []
    for step in range(1, n):
        target = lax.rem(me + step, n)
        src = part_ref.at[:, pl.ds(pl.multiple_of(target * chunk, 128), chunk)]
        copy = push("obs", n, me, step, src, landed.at[step], send_a, recv_a)
        copy.start()
        copies.append(copy)
    total = part_ref[:, pl.ds(pl.multiple_of(me * chunk, 128), chunk)]
    for step in range(1, n):
        copies[step - 1].wait()
        total = total + landed[step]
    if mode == 0:
        residual = total
        direction = residual / keep_ref[...]
        solution = direction
    else:
        direction = dir_ref[...]
        residual = res_ref[...] - (total + shift_ref[...] * direction)
        direction = keep_ref[...] * direction + gain_ref[...] * residual
        solution = sol_ref[...] + direction
    res_out[...] = residual
    dir_out[...] = direction
    sol_out[...] = solution
    sent = solution if mode == 2 else direction
    gathered[0] = sent.astype(jnp.bfloat16)
    copies = []
    for step in range(1, n):
        copy = push("obs", n, me, step, gathered.at[0], gathered.at[step], send_b, recv_b)
        copy.start()
        copies.append(copy)
    for step in range(n):
        if step:
            copies[step - 1].wait()
        origin = lax.rem(me + n - step, n)
        full_out[:, pl.ds(pl.multiple_of(origin * chunk, 128), chunk)] = gathered[step]


def normal_exchange(mode, n, partial, residual, direction, solution, shift, keep, gain):
    chunk = residual.shape[1]
    shard = jax.ShapeDtypeStruct((COLS, chunk), jnp.float32)
    return pl.pallas_call(
        functools.partial(normal_kernel, n, mode),
        out_shape=(shard, shard, shard, jax.ShapeDtypeStruct(partial.shape, jnp.bfloat16)),
        in_specs=[VMEM_SPEC] * 7,
        out_specs=(VMEM_SPEC,) * 4,
        scratch_shapes=[
            pltpu.VMEM((n, COLS, chunk), jnp.float32),
            pltpu.VMEM((n, COLS, chunk), jnp.bfloat16),
        ]
        + [pltpu.SemaphoreType.DMA((n,))] * 4,
        compiler_params=pltpu.CompilerParams(collective_id=mode, has_side_effects=True),
        name="normal_exchange",
    )(partial, residual, direction, solution, shift, keep, gain)


def sum_kernel(n, x_ref, o_ref, landed, send_sem, recv_sem):
    me = lax.axis_index("coef")
    greet("coef", n, me)
    copies = []
    for step in range(1, n):
        copy = push("coef", n, me, step, x_ref, landed.at[step], send_sem, recv_sem)
        copy.start()
        copies.append(copy)
    total = x_ref[...]
    for step in range(1, n):
        copies[step - 1].wait()
        total = total + landed[step]
    o_ref[...] = total.astype(o_ref.dtype)


def coef_sum(partial, n, cid):
    return pl.pallas_call(
        functools.partial(sum_kernel, n),
        out_shape=jax.ShapeDtypeStruct(partial.shape, jnp.bfloat16),
        in_specs=[VMEM_SPEC],
        out_specs=VMEM_SPEC,
        scratch_shapes=[pltpu.VMEM((n,) + partial.shape, jnp.float32)]
        + [pltpu.SemaphoreType.DMA((n,))] * 2,
        compiler_params=pltpu.CompilerParams(collective_id=cid, has_side_effects=True),
        name="coef_sum",
    )(partial)


def scatter_kernel(n, x_ref, o_ref, landed, send_sem, recv_sem):
    me = lax.axis_index("coef")
    greet("coef", n, me)
    copies = []
    for step in range(1, n):
        target = lax.rem(me + step, n)
        copy = push("coef", n, me, step, x_ref.at[target], landed.at[step], send_sem, recv_sem)
        copy.start()
        copies.append(copy)
    total = x_ref[me].astype(jnp.float32)
    for step in range(1, n):
        copies[step - 1].wait()
        total = total + landed[step].astype(jnp.float32)
    o_ref[...] = total


def coef_scatter(parts, n, cid):
    return pl.pallas_call(
        functools.partial(scatter_kernel, n),
        out_shape=jax.ShapeDtypeStruct(parts.shape[1:], jnp.float32),
        in_specs=[VMEM_SPEC],
        out_specs=VMEM_SPEC,
        scratch_shapes=[pltpu.VMEM(parts.shape, parts.dtype)]
        + [pltpu.SemaphoreType.DMA((n,))] * 2,
        compiler_params=pltpu.CompilerParams(collective_id=cid, has_side_effects=True),
        name="coef_scatter",
    )(parts)


def place_kernel(width, row_ref, col_ref, sol_ref, out_ref, spread):
    out_ref[...] = jnp.zeros_like(out_ref)
    wide = jnp.zeros((COLS, width), jnp.int32)

    def step(index, carry):
        at = pl.ds(pl.multiple_of(index * width, 128), width)
        values = sol_ref[:, at].astype(jnp.float32)
        rows = row_ref[:, at] + wide
        for pair in range(NL // 2):
            first = jnp.where(rows == 2 * pair, values, 0.0)
            second = jnp.where(rows == 2 * pair + 1, values, 0.0)
            both = jnp.concatenate([first, second], axis=0)
            spread[pair * 2 * COLS : (pair + 1) * 2 * COLS, :] = both.astype(jnp.bfloat16)
        degree = lax.broadcasted_iota(jnp.int32, (NL, width), 0)
        hot = jnp.where(degree == col_ref[:, at], 1.0, 0.0).astype(jnp.bfloat16)
        out_ref[...] += lax.dot_general(
            spread[...], hot, (((1,), (1,)), ((), ())), preferred_element_type=jnp.float32
        )
        return carry

    lax.fori_loop(0, sol_ref.shape[1] // width, step, 0)


def place(rows, cols, sol):
    kdev = sol.shape[1]
    width = next(w for w in (512, 384, 256, 128) if kdev % w == 0)
    return pl.pallas_call(
        functools.partial(place_kernel, width),
        out_shape=jax.ShapeDtypeStruct((NL * COLS, NL), jnp.float32),
        in_specs=[VMEM_SPEC] * 3,
        out_specs=VMEM_SPEC,
        scratch_shapes=[pltpu.VMEM((NL * COLS, width), jnp.bfloat16)],
        compiler_params=pltpu.CompilerParams(vmem_limit_bytes=32 << 20),
        name="place",
    )(rows, cols, sol)


def table_of(level, order, valid):
    product = (level - order) * (level + order)
    denom = jnp.where(valid, product, 1.0)
    first = jnp.sqrt(jnp.maximum((2.0 * level - 1.0) * (2.0 * level + 1.0), 0.0) / denom)
    second = jnp.sqrt(
        jnp.maximum((2.0 * level + 1.0) * (level + order - 1.0) * (level - order - 1.0), 0.0)
        / (denom * jnp.maximum(2.0 * level - 3.0, 1.0))
    )
    return jnp.where(valid, first, 0.0), jnp.where(valid, second, 0.0)


def legendre_kernel(order_ref, cos_ref, sin_ref, w_ref, out_ref, a_c, b_c, a_s, b_s, grow):
    lats, lanes = cos_ref.shape
    order = order_ref[0:1, :]
    other = float(NL) - order
    count = lax.broadcasted_iota(jnp.int32, (NL, lanes), 0).astype(jnp.float32)
    wide = jnp.zeros((NL, lanes), jnp.float32)
    low = order + wide
    high = other + wide
    level = count + low
    a, b = table_of(level, low, jnp.logical_and(count > 0.0, level < float(NL)))
    a_c[...] = a
    b_c[...] = b
    a, b = table_of(count, high, count > high)
    a_s[...] = a
    b_s[...] = b
    safe = jnp.maximum(count, 1.0)
    grow[...] = jnp.where(
        count == 1.0, math.sqrt(3.0), jnp.sqrt((2.0 * safe + 1.0) / (2.0 * safe))
    )
    cosine = cos_ref[...]
    sine = sin_ref[...]
    zero = cosine * 0.0
    low = order_ref[...]
    high = float(NL) - low

    def climb(degree, carry):
        diag, dc, ds = carry
        diag = diag * sine * grow[pl.ds(degree, 1), :]
        here = degree.astype(jnp.float32)
        return diag, jnp.where(low == here, diag, dc), jnp.where(high == here, diag, ds)

    start = zero + 1.0
    _, dc, ds = lax.fori_loop(
        1, NL, climb, (start, jnp.where(low == 0.0, start, zero), zero), unroll=4
    )
    acc_c = dc * w_ref[pl.ds(0, 1), :]

    def advance(column, carry):
        pc, ec, ps, es, acc_c, acc_s = carry
        at = pl.ds(column, 1)
        w = w_ref[at, :]
        vc = a_c[at, :] * cosine * pc - b_c[at, :] * ec
        begin = jnp.where(high == column.astype(jnp.float32), ds, 0.0)
        vs = a_s[at, :] * cosine * ps - b_s[at, :] * es + begin
        return vc, pc, vs, ps, acc_c + vc * w, acc_s + vs * w

    _, _, _, _, acc_c, acc_s = lax.fori_loop(
        1, NL, advance, (dc, zero, zero, zero, acc_c, zero), unroll=4
    )
    out_ref[0] = acc_c / math.sqrt(NL)
    out_ref[1] = acc_s / math.sqrt(NL)


def legendre(orders, colatitude, w):
    lanes = w.shape[1]
    lats = colatitude.shape[0]
    spread = jnp.zeros((lats, lanes), jnp.float32)
    table = pltpu.VMEM((NL, lanes), jnp.float32)
    return pl.pallas_call(
        legendre_kernel,
        out_shape=jax.ShapeDtypeStruct((2, lats, lanes), jnp.float32),
        in_specs=[VMEM_SPEC] * 4,
        out_specs=VMEM_SPEC,
        scratch_shapes=[table] * 5,
        name="legendre",
    )(
        orders[None, :] + spread,
        jnp.cos(colatitude)[:, None] + spread,
        jnp.sin(colatitude)[:, None] + spread,
        w,
    )


def wave_tables(rows, longitudes):
    steps_k = jnp.arange(longitudes, dtype=jnp.int32)
    scale = 2.0 * math.pi / longitudes
    cos_angle = (rows[:, None] * steps_k[None, :] % longitudes).astype(jnp.float32) * scale
    sin_angle = ((NL - rows)[:, None] * steps_k[None, :] % longitudes).astype(jnp.float32) * scale
    return (jnp.cos(cos_angle), jnp.sin(sin_angle))


def body(design, observations, shift_table, shift_index, coef_perm, order_map):
    obs_count = lax.axis_size("obs")
    coef_count = lax.axis_size("coef")
    coef_rank = lax.axis_index("coef")
    obs_rank = lax.axis_index("obs")
    kdev = design.shape[1]
    chunk = kdev // obs_count
    direct = chunk % 128 == 0
    table_index = jnp.arange(NSHIFT, dtype=jnp.int32)
    shifts = jnp.sum(
        jnp.where(shift_index[:, None] == table_index[None, :], shift_table[None, :], 0.0), axis=1
    )
    centre = shifts + CENTRE_OFFSET
    ratio_start = centre / HALF_WIDTH

    if direct:
        residual = direction = solution = jnp.zeros((COLS, chunk), jnp.float32)

    def exchange(mode, partial, state, keep, gain):
        residual, direction, solution = state
        if direct:
            residual, direction, solution, full = normal_exchange(
                mode, obs_count, partial, residual, direction, solution,
                shifts[:, None], keep[:, None], gain[:, None],
            )
            return (residual, direction, solution), full
        total = lax.psum(partial, "obs")
        if mode == 0:
            residual = total
            direction = residual / keep[:, None]
            solution = direction
        else:
            residual = residual - (total + shifts[:, None] * direction)
            direction = keep[:, None] * direction + gain[:, None] * residual
            solution = solution + direction
        full = solution if mode == 2 else direction
        return (residual, direction, solution), full.astype(jnp.bfloat16)

    empty = jnp.zeros((COLS, chunk if direct else kdev), jnp.float32)
    rhs = jnp.dot(observations, design, preferred_element_type=jnp.float32)
    state, full = exchange(0, rhs, (empty, empty, empty), centre, centre)
    factor = 1.0 / ratio_start
    for iteration in range(ITERS):
        partial_image = lax.dot_general(
            full, design, (((1,), (1,)), ((), ())), preferred_element_type=jnp.float32
        )
        image = coef_sum(partial_image, coef_count, 3 + iteration)
        partial = jnp.dot(image, design, preferred_element_type=jnp.float32)
        factor_next = 1.0 / (2.0 * ratio_start - factor)
        last = iteration == ITERS - 1
        state, full = exchange(
            2 if last else 1, partial, state, factor_next * factor, 2.0 * factor_next / HALF_WIDTH
        )
        factor = factor_next
    block_count = coef_count * BPO
    block_rows = NL // block_count
    owned_rows = kdev // NL
    block_ids = jnp.arange(block_count, dtype=jnp.int32)
    position = jnp.sum(
        jnp.where(order_map[:, None] == block_ids[None, :], block_ids[:, None], 0), axis=0
    )
    paired_row = coef_perm // NL
    column = coef_perm % NL
    place_of = jnp.sum(
        jnp.where(
            (paired_row // block_rows)[None, :] == block_ids[:, None], position[:, None], 0
        ),
        axis=0,
    )
    owner_row = place_of * block_rows + paired_row % block_rows
    placed = place(owner_row[None, :], column[None, :], full)
    lanes = owned_rows * COLS
    outgoing = placed.astype(jnp.bfloat16).reshape(coef_count, lanes, NL)
    local = coef_scatter(outgoing, coef_count, 5).T
    my_blocks = lax.dynamic_slice_in_dim(order_map, coef_rank * BPO, BPO)
    row_offsets = jnp.arange(block_rows, dtype=jnp.int32)
    owned_canon = (my_blocks[:, None] * block_rows + row_offsets[None, :]).reshape(owned_rows)
    lat_block = LAT_DEV * coef_count
    lat_total = lat_block * obs_count
    lat_ids = obs_rank * lat_block + jnp.arange(lat_block, dtype=jnp.int32)
    colatitude = math.pi * (lat_ids.astype(jnp.float32) + 0.5) / lat_total
    orders = jnp.repeat(owned_canon, COLS).astype(jnp.float32)
    parts = legendre(orders, colatitude, local).reshape(2, lat_block, owned_rows, COLS)
    band = parts.transpose(2, 0, 3, 1)
    own_cos, own_sin = wave_tables(owned_canon, NLON)
    first_sum = jnp.einsum("lqc,qk->lck", parts[0], own_cos, precision=lax.Precision.HIGHEST)
    second_sum = jnp.einsum("lqc,qk->lck", parts[1], own_sin, precision=lax.Precision.HIGHEST)
    shares = ((first_sum + second_sum) / math.sqrt(NL)).reshape(
        coef_count, LAT_DEV * COLS, NLON
    )
    field = coef_scatter(shares, coef_count, 6).reshape(LAT_DEV, COLS, NLON).transpose(1, 0, 2)
    return (band, field)


def solution(mesh):
    placed = (P("obs", "coef"), P(None, "obs"), P(), P(), P("coef"), P())
    return jax.shard_map(
        body,
        mesh=mesh,
        in_specs=placed,
        out_specs=(P("coef", None, None, "obs"), P(None, ("obs", "coef"), None)),
        check_vma=False,
    )
```

time: 906 us -> 171 us (0.19)
  loops' own time: 363 us -> 0 us
  local copies, waits for them, and re-layouts: 245 us -> 9.53 us
  waiting for transfers between devices: 165 us -> 0 us
  Pallas kernels: 0 us -> 100 us
  other arithmetic: 26.6 us -> 3.02 us
  blocking collectives: 22.2 us -> 0 us
  between operations: 14 us -> 0.81 us
    another operation x1 -> x0, loops' own time: 363 us -> none  [legendre_table(): lax.scan(advance, (jnp.zeros_like(sine), start, start), jnp.arange(degree...]
    psum x3 -> x0, waiting for transfers between devices: 142 us -> none  [reduce_normal(): return lax.psum(partial_normal, 'obs')]
    gather x3 -> x0, local copies, waits for them, and re-layouts: 138 us -> none  [body(): shifted = jnp.take_along_axis(local, roll_index[None, :, :], axis=2)]
    pallas_call x0 -> x9, Pallas kernels: none -> 100 us  [the longest x3 55.5 us: normal_exchange(): pl.pallas_call(functools.partial(normal_kernel, n, mode), out_shape=(shar...]
    scatter x3 -> x0, local copies, waits for them, and re-layouts: 86.2 us -> none  [the longest x1 34.8 us: body(): labels = jnp.zeros((kdev,), jnp.float32).at[slot].set(coef_perm.astype(jn...]
    psum x2 -> x0, blocking collectives: 22.2 us -> none  [body(): image = lax.psum(partial_image, 'coef')]
    reduce_scatter x1 -> x0, waiting for transfers between devices: 17.3 us -> none  [body(): lax.psum_scatter((first_sum + second_sum) / math.sqrt(NL), 'coef', scatte...]
    while x180 -> x0, other arithmetic: 14.2 us -> none
  transfers between devices with their start and end apart: 6 -> 0, of which waited for: 4 -> 0; matrix products, arithmetic and copies ran while one was open for 7% -> 0% of each run, Pallas kernels for 0% -> 0%
where the time goes in v1:
time: 171 us; the launch traced here: 170 us
  Pallas kernels  100 us (58%)
  matrix products  56 us (33%)
  local copies, waits for them, and re-layouts  9.53 us (6%)
  other arithmetic  3.02 us (2%)
    pallas_call x3, Pallas kernels, normal_exchange(): pl.pallas_call(functools.partial(normal_kernel, n, mode), out_shape=(shar...  55.5 us
    dot_general x2, matrix products, body(): lax.dot_general(full, design, (((1,), (1,)), ((), ())), preferred_element...  24.3 us
    dot_general x2, matrix products, body(): partial = jnp.dot(image, design, preferred_element_type=jnp.float32)  19.3 us
    pallas_call x2, Pallas kernels, coef_scatter(): pl.pallas_call(functools.partial(scatter_kernel, n), out_shape=jax.ShapeD...  18.5 us
    pallas_call x2, Pallas kernels, coef_sum(): pl.pallas_call(functools.partial(sum_kernel, n), out_shape=jax.ShapeDtype...  10.9 us
    pallas_call x1, Pallas kernels, place(): pl.pallas_call(functools.partial(place_kernel, width), out_shape=jax.Shap...  10.8 us
    dot_general x1, matrix products, body(): rhs = jnp.dot(observations, design, preferred_element_type=jnp.float32)  9.63 us
    pallas_call x1, Pallas kernels, legendre(): pl.pallas_call(legendre_kernel, out_shape=jax.ShapeDtypeStruct((2, lats,...  4.63 us

profile of v1, /device:TPU:0, one launch (start us, length us, event | category | flops | bytes accessed | tf_op | source)
XLA Modules:
  0.0 169.8 jit_solution(15600183613590333254)
XLA Ops:
  0.6 0.0 copy-start
  0.6 0.9 select_reduce_fusion.1
  1.5 0.1 copy.27.shift_ref
  1.6 0.6 broadcast_multiply_fusion
  2.2 0.0 copy-done
  2.2 9.6 %fusion.50.part_ref = f32[8,9216]{1,0:T(8,128)} fusion(bf16[8,1024]{1,0:T(8,128)(2,1)S(1)} %copy-done, bf16[1024,9216]{1,0:T(8,128)(2,1)} %param.6), kind=kOutput, calls=%fused_computation.75 | convolution fusion | flops 150994944 | bytes 19185664 | tf_op jit(solution)/shard_map/dot_general | solution.py:333
  11.8 0.6 broadcast_in_dim.53.res_ref.dir_ref.sol_ref
  12.5 0.0 copy-done.3
  12.5 20.5 %normal_exchange.3 = (f32[8,1152]{1,0:T(8,128)}, f32[8,1152]{1,0:T(8,128)}, f32[8,1152]{1,0:T(8,128)}, bf16[8,9216]{1,0:T(8,128)(2,1)}) custom-call(f32[8,9216]{1,0:T(8,128)} %fusion.50.part_ref, f32[8,1152]{1,0:T(8,128)} %broadcast_in_dim.53.res_ref.dir_ref.sol_ref, f32[8,1152]{1,0:T(8,128)} %broadcast_in_dim.53.res_ref.dir_ref.sol_ref, ...), custom_call_target="tpu_custom_call" | custom-call | tf_op jit(solution)/shard_map/normal_exchange/pallas_call | solution.py:93
  32.9 12.0 %fusion.51.x_ref = f32[8,1024]{1,0:T(8,128)} fusion(bf16[8,9216]{1,0:T(8,128)(2,1)} %get-tuple-element.11, bf16[1024,9216]{1,0:T(8,128)(2,1)} %param.6), kind=kOutput, calls=%fused_computation.76 | convolution fusion | flops 150994944 | bytes 19054592 | tf_op jit(solution)/shard_map/dot_general | solution.py:337
  45.0 5.5 %coef_sum.2 = bf16[8,1024]{1,0:T(8,128)(2,1)} custom-call(f32[8,1024]{1,0:T(8,128)} %fusion.51.x_ref), custom_call_target="tpu_custom_call" | custom-call | tf_op jit(solution)/shard_map/coef_sum/pallas_call | solution.py:124
  50.4 9.6 %fusion.52.part_ref = f32[8,9216]{1,0:T(8,128)} fusion(bf16[8,1024]{1,0:T(8,128)(2,1)} %coef_sum.2, bf16[1024,9216]{1,0:T(8,128)(2,1)} %param.6), kind=kOutput, calls=%fused_computation.77 | convolution fusion | flops 150994944 | bytes 19185664 | tf_op jit(solution)/shard_map/dot_general | solution.py:341
  60.1 17.4 %normal_exchange.4 = (f32[8,1152]{1,0:T(8,128)}, f32[8,1152]{1,0:T(8,128)}, f32[8,1152]{1,0:T(8,128)}, bf16[8,9216]{1,0:T(8,128)(2,1)}) custom-call(f32[8,9216]{1,0:T(8,128)} %fusion.52.part_ref, f32[8,1152]{1,0:T(8,128)} %get-tuple-element.12.res_ref, f32[8,1152]{1,0:T(8,128)} %get-tuple-element.13.dir_ref, f32[8,1152]{1,0:T(8,128)} %get-tuple-element.14.sol_ref, ...), custom_call_target="tpu_custom_call" | custom-call | tf_op jit(solution)/shard_map/normal_exchange/pallas_call | solution.py:93
  77.5 0.0 copy-start.2
  77.5 0.0 copy-start.4
  77.5 12.2 %fusion.53.x_ref = f32[8,1024]{1,0:T(8,128)} fusion(bf16[8,9216]{1,0:T(8,128)(2,1)} %get-tuple-element.15, bf16[1024,9216]{1,0:T(8,128)(2,1)} %param.6), kind=kOutput, calls=%fused_computation.78 | convolution fusion | flops 150994944 | bytes 19054592 | tf_op jit(solution)/shard_map/dot_general | solution.py:337
  89.8 5.5 %coef_sum.3 = bf16[8,1024]{1,0:T(8,128)(2,1)} custom-call(f32[8,1024]{1,0:T(8,128)} %fusion.53.x_ref), custom_call_target="tpu_custom_call" | custom-call | tf_op jit(solution)/shard_map/coef_sum/pallas_call | solution.py:124
  95.2 9.6 %fusion.54.part_ref = f32[8,9216]{1,0:T(8,128)} fusion(bf16[8,1024]{1,0:T(8,128)(2,1)} %coef_sum.3, bf16[1024,9216]{1,0:T(8,128)(2,1)} %param.6), kind=kOutput, calls=%fused_computation.79 | convolution fusion | flops 150994944 | bytes 19185664 | tf_op jit(solution)/shard_map/dot_general | solution.py:341
  104.9 17.6 %normal_exchange.5 = (f32[8,1152]{1,0:T(8,128)}, f32[8,1152]{1,0:T(8,128)}, f32[8,1152]{1,0:T(8,128)}, bf16[8,9216]{1,0:T(8,128)(2,1)}) custom-call(f32[8,9216]{1,0:T(8,128)} %fusion.54.part_ref, f32[8,1152]{1,0:T(8,128)} %get-tuple-element.16.res_ref, f32[8,1152]{1,0:T(8,128)} %get-tuple-element.17.dir_ref, f32[8,1152]{1,0:T(8,128)} %get-tuple-element.18.sol_ref, ...), custom_call_target="tpu_custom_call" | custom-call | tf_op jit(solution)/shard_map/normal_exchange/pallas_call | solution.py:93
  122.5 0.0 copy-done.2
  122.6 0.1 add_select_fusion.4
  122.6 0.0 copy-done.4
  122.6 0.1 select_reduce_fusion.2
  122.7 0.2 select_reduce_fusion
  122.9 0.1 add_select_fusion.2
  123.0 0.9 copy-done.1
  123.9 10.8 %place.1 = f32[1536,192]{1,0:T(8,128)S(1)} custom-call(s32[1,9216]{1,0:T(1,128)S(1)} %bitcast.26, s32[1,9216]{1,0:T(1,128)S(1)} %bitcast.25, bf16[8,9216]{1,0:T(8,128)(2,1)S(1)} %copy-done.1), custom_call_target="tpu_custom_call" | custom-call | tf_op jit(solution)/shard_map/place/pallas_call | solution.py:191
  134.7 1.0 convert_element_type.33
  135.7 12.4 %coef_scatter.2 = f32[384,192]{1,0:T(8,128)} custom-call(bf16[4,384,192]{2,1,0:T(8,128)(2,1)} %bitcast.27), custom_call_target="tpu_custom_call" | custom-call | tf_op jit(solution)/shard_map/coef_scatter/pallas_call | solution.py:153
  148.1 1.9 %copy.30 = f32[384,192]{0,1:T(8,128)} copy(f32[384,192]{1,0:T(8,128)} %coef_scatter.2) | data formatting | bytes 589824 | tf_op jit(solution)/shard_map/coef_scatter/pallas_call | solution.py:153
  150.0 0.1 dynamic-slice_multiply_fusion
  150.0 0.1 iota_add_fusion
  150.1 0.1 add.123
  150.2 0.1 broadcast_in_dim.46
  150.3 0.1 convert_element_type.31
  150.4 0.6 add.124.order_ref
  151.0 0.7 add.128.cos_ref
  151.7 0.7 add.129.sin_ref
  152.3 4.6 %legendre.1 = f32[2,4,384]{2,1,0:T(4,128)} custom-call(f32[4,384]{1,0:T(4,128)} %add.124.order_ref, f32[4,384]{1,0:T(4,128)} %add.128.cos_ref, f32[4,384]{1,0:T(4,128)} %add.129.sin_ref, f32[192,384]{1,0:T(8,128)} %bitcast.28), custom_call_target="tpu_custom_call" | custom-call | tf_op jit(solution)/shard_map/legendre/pallas_call | solution.py:271
  157.0 0.7 fusion.49
  157.7 0.1 squeeze.6
  157.8 1.1 fusion.6
  158.9 0.1 squeeze.7
  159.0 1.7 %fusion.x_ref = f32[4,8,1024]{2,1,0:T(8,128)} fusion(f32[4,8,1024]{2,1,0:T(8,128)S(1)} %fusion.6, f32[4,48,8]{2,1,0:T(8,128)S(1)} %squeeze.7, s32[48]{0:T(128)S(1)} %get-tuple-element.35), kind=kOutput, calls=%fused_computation.1 | convolution fusion | flops 19628032 | bytes 268480 | tf_op jit(solution)/shard_map/lqc,qk->lck/dot_general | solution.py:380
  160.7 6.1 %coef_scatter.3 = f32[8,1024]{1,0:T(8,128)} custom-call(f32[4,8,1024]{2,1,0:T(8,128)} %fusion.x_ref), custom_call_target="tpu_custom_call" | custom-call | tf_op jit(solution)/shard_map/coef_scatter/pallas_call | solution.py:153
  166.8 1.4 copy.34
  168.2 0.8 reshape.120
  169.0 0.7 copy.33
  (4 shorter events, 0.1 us)
Async XLA Ops:
  0.6 1.6 copy-start
  1.6 10.9 %copy-start.3 = (f32[8,1]{1,0:T(8,128)}, f32[8,1]{1,0:T(8,128)S(1)}, u32[]{:S(2)}) copy-start(f32[8,1]{1,0:T(8,128)S(1)} %copy.27.shift_ref) | copy-start | bytes 100
  77.5 45.0 %copy-start.2 = (s32[9216]{0:T(1024)S(1)}, s32[9216]{0:T(1024)}, u32[]{:S(2)}) copy-start(s32[9216]{0:T(1024)} %param.10) | copy-start | bytes 110596
  77.5 45.1 %copy-start.4 = (s32[8]{0:T(128)S(1)}, s32[8]{0:T(128)}, u32[]{:S(2)}) copy-start(s32[8]{0:T(128)} %param.11) | copy-start | bytes 100
  123.0 0.9 copy-start.1

commit v2 on v1

--- a/solution.py
+++ b/solution.py
@@ -42,67 +42,142 @@
     )
 
 
-def normal_kernel(
-    n, mode, part_ref, res_ref, dir_ref, sol_ref, shift_ref, keep_ref, gain_ref,
-    res_out, dir_out, sol_out, full_out,
-    landed, gathered, send_a, recv_a, send_b, recv_b,
+def solver_kernel(
+    n, nc, obs_ref, design_ref, shift_ref, keep_ref, gain_ref, full_out,
+    held, part, landed, gathered, image_sent, image_landed,
+    load_sem, send_a, recv_a, send_b, recv_b, send_c, recv_c,
 ):
     me = lax.axis_index("obs")
-    chunk = res_ref.shape[1]
-    greet("obs", n, me)
-    copies = []
-    for step in range(1, n):
-        target = lax.rem(me + step, n)
-        src = part_ref.at[:, pl.ds(pl.multiple_of(target * chunk, 128), chunk)]
-        copy = push("obs", n, me, step, src, landed.at[step], send_a, recv_a)
-        copy.start()
-        copies.append(copy)
-    total = part_ref[:, pl.ds(pl.multiple_of(me * chunk, 128), chunk)]
-    for step in range(1, n):
-        copies[step - 1].wait()
-        total = total + landed[step]
-    if mode == 0:
-        residual = total
-        direction = residual / keep_ref[...]
-        solution = direction
-    else:
-        direction = dir_ref[...]
-        residual = res_ref[...] - (total + shift_ref[...] * direction)
-        direction = keep_ref[...] * direction + gain_ref[...] * residual
-        solution = sol_ref[...] + direction
-    res_out[...] = residual
-    dir_out[...] = direction
-    sol_out[...] = solution
-    sent = solution if mode == 2 else direction
-    gathered[0] = sent.astype(jnp.bfloat16)
-    copies = []
-    for step in range(1, n):
-        copy = push("obs", n, me, step, gathered.at[0], gathered.at[step], send_b, recv_b)
-        copy.start()
-        copies.append(copy)
+    mine = lax.axis_index("coef")
+    chunk = part.shape[2]
+
+    def load(step):
+        block = lax.rem(me + step, n)
+        return pltpu.make_async_copy(
+            design_ref.at[:, pl.ds(pl.multiple_of(block * chunk, 128), chunk)],
+            held.at[step],
+            load_sem.at[step],
+        )
+
+    for step in list(range(1, n)) + [0]:
+        load(step).start()
+    barrier = pltpu.get_barrier_semaphore()
+    for axis, count, rank in (("obs", n, me), ("coef", nc, mine)):
+        for step in range(1, count):
+            pl.semaphore_signal(
+                barrier,
+                inc=1,
+                device_id={axis: lax.rem(rank + step, count)},
+                device_id_type=MESH,
+            )
+    pl.semaphore_wait(barrier, n + nc - 2)
+
+    def scatter_copy(rnd, step):
+        return push(
+            "obs", n, me, step, part.at[step], landed.at[rnd, step], send_a.at[rnd], recv_a.at[rnd]
+        )
+
+    def gather_copy(rnd, step):
+        return push(
+            "obs", n, me, step, gathered.at[rnd, 0], gathered.at[rnd, step],
+            send_b.at[rnd], recv_b.at[rnd],
+        )
+
+    def image_copy(rnd, step):
+        return push(
+            "coef", nc, mine, step, image_sent, image_landed.at[rnd, step],
+            send_c.at[rnd], recv_c.at[rnd],
+        )
+
+    def transposed_pass(rnd, left):
+        def compute(step, carry):
+            if rnd == 0:
+                load(step).wait()
+            part[step] = jnp.dot(left, held[step], preferred_element_type=jnp.float32)
+            scatter_copy(rnd, step).start()
+            return carry
+
+        lax.fori_loop(1, n, compute, 0)
+        if rnd == 0:
+            load(0).wait()
+        total = jnp.dot(left, held[0], preferred_element_type=jnp.float32)
+        for step in range(1, n):
+            scatter_copy(rnd, step).wait()
+            total = total + landed[rnd, step]
+        return total
+
+    def gather(rnd, value):
+        gathered[rnd, 0] = value.astype(jnp.bfloat16)
+        for step in range(1, n):
+            gather_copy(rnd, step).start()
+
+    def image_of(rnd):
+        image_sent[...] = jnp.zeros_like(image_sent)
+
+        def compute(step, carry):
+            @pl.when(step > 0)
+            def _():
+                gather_copy(rnd, step).wait()
+
+            image_sent[...] += lax.dot_general(
+                gathered[rnd, step],
+                held[lax.rem(n - step, n)],
+                (((1,), (1,)), ((), ())),
+                preferred_element_type=jnp.float32,
+            )
+            return carry
+
+        lax.fori_loop(0, n, compute, 0)
+        for step in range(1, nc):
+            image_copy(rnd, step).start()
+        image = image_sent[...]
+        for step in range(1, nc):
+            image_copy(rnd, step).wait()
+            image = image + image_landed[rnd, step]
+        return image.astype(jnp.bfloat16)
+
+    residual = transposed_pass(0, obs_ref[...])
+    direction = residual / keep_ref[0]
+    solution = direction
+    gather(0, direction)
+    for rnd in range(1, ITERS + 1):
+        total = transposed_pass(rnd, image_of(rnd - 1))
+        residual = residual - (total + shift_ref[...] * direction)
+        direction = keep_ref[rnd] * direction + gain_ref[rnd] * residual
+        solution = solution + direction
+        gather(rnd, solution if rnd == ITERS else direction)
     for step in range(n):
         if step:
-            copies[step - 1].wait()
+            gather_copy(ITERS, step).wait()
         origin = lax.rem(me + n - step, n)
-        full_out[:, pl.ds(pl.multiple_of(origin * chunk, 128), chunk)] = gathered[step]
-
-
-def normal_exchange(mode, n, partial, residual, direction, solution, shift, keep, gain):
-    chunk = residual.shape[1]
-    shard = jax.ShapeDtypeStruct((COLS, chunk), jnp.float32)
+        full_out[:, pl.ds(pl.multiple_of(origin * chunk, 128), chunk)] = gathered[ITERS, step]
+
+
+def solve(n, nc, observations, design, shift, keep, gain):
+    rows, kdev = design.shape
+    chunk = kdev // n
+    rounds = ITERS + 1
     return pl.pallas_call(
-        functools.partial(normal_kernel, n, mode),
-        out_shape=(shard, shard, shard, jax.ShapeDtypeStruct(partial.shape, jnp.bfloat16)),
-        in_specs=[VMEM_SPEC] * 7,
-        out_specs=(VMEM_SPEC,) * 4,
+        functools.partial(solver_kernel, n, nc),
+        out_shape=jax.ShapeDtypeStruct((COLS, kdev), jnp.bfloat16),
+        in_specs=[VMEM_SPEC, pl.BlockSpec(memory_space=pl.ANY)] + [VMEM_SPEC] * 3,
+        out_specs=VMEM_SPEC,
         scratch_shapes=[
+            pltpu.VMEM((n, rows, chunk), jnp.bfloat16),
             pltpu.VMEM((n, COLS, chunk), jnp.float32),
-            pltpu.VMEM((n, COLS, chunk), jnp.bfloat16),
+            pltpu.VMEM((rounds, n, COLS, chunk), jnp.float32),
+            pltpu.VMEM((rounds, n, COLS, chunk), jnp.bfloat16),
+            pltpu.VMEM((COLS, rows), jnp.float32),
+            pltpu.VMEM((ITERS, nc, COLS, rows), jnp.float32),
+            pltpu.SemaphoreType.DMA((n,)),
         ]
-        + [pltpu.SemaphoreType.DMA((n,))] * 4,
-        compiler_params=pltpu.CompilerParams(collective_id=mode, has_side_effects=True),
-        name="normal_exchange",
-    )(partial, residual, direction, solution, shift, keep, gain)
+        + [pltpu.SemaphoreType.DMA((rounds, n))] * 4
+        + [pltpu.SemaphoreType.DMA((ITERS, nc))] * 2,
+        compiler_params=pltpu.CompilerParams(
+            collective_id=0, has_side_effects=True, vmem_limit_bytes=48 << 20
+        ),
+        name="solve",
+    )(observations, design, shift, keep, gain)
 
 
 def sum_kernel(n, x_ref, o_ref, landed, send_sem, recv_sem):
@@ -131,6 +206,27 @@
         compiler_params=pltpu.CompilerParams(collective_id=cid, has_side_effects=True),
         name="coef_sum",
     )(partial)
+
+
+def solve_plain(nc, observations, design, shift, keep, gain):
+    def transposed_pass(left):
+        return lax.psum(jnp.dot(left, design, preferred_element_type=jnp.float32), "obs")
+
+    residual = transposed_pass(observations)
+    direction = residual / keep[0]
+    solution = direction
+    for rnd in range(1, ITERS + 1):
+        partial_image = lax.dot_general(
+            direction.astype(jnp.bfloat16),
+            design,
+            (((1,), (1,)), ((), ())),
+            preferred_element_type=jnp.float32,
+        )
+        total = transposed_pass(coef_sum(partial_image, nc, 2 + rnd))
+        residual = residual - (total + shift * direction)
+        direction = keep[rnd] * direction + gain[rnd] * residual
+        solution = solution + direction
+    return solution.astype(jnp.bfloat16)
 
 
 def scatter_kernel(n, x_ref, o_ref, landed, send_sem, recv_sem):
@@ -306,45 +402,22 @@
     centre = shifts + CENTRE_OFFSET
     ratio_start = centre / HALF_WIDTH
 
-    if direct:
-        residual = direction = solution = jnp.zeros((COLS, chunk), jnp.float32)
-
-    def exchange(mode, partial, state, keep, gain):
-        residual, direction, solution = state
-        if direct:
-            residual, direction, solution, full = normal_exchange(
-                mode, obs_count, partial, residual, direction, solution,
-                shifts[:, None], keep[:, None], gain[:, None],
-            )
-            return (residual, direction, solution), full
-        total = lax.psum(partial, "obs")
-        if mode == 0:
-            residual = total
-            direction = residual / keep[:, None]
-            solution = direction
-        else:
-            residual = residual - (total + shifts[:, None] * direction)
-            direction = keep[:, None] * direction + gain[:, None] * residual
-            solution = solution + direction
-        full = solution if mode == 2 else direction
-        return (residual, direction, solution), full.astype(jnp.bfloat16)
-
-    empty = jnp.zeros((COLS, chunk if direct else kdev), jnp.float32)
-    rhs = jnp.dot(observations, design, preferred_element_type=jnp.float32)
-    state, full = exchange(0, rhs, (empty, empty, empty), centre, centre)
+    keep = [centre]
+    gain = [centre]
     factor = 1.0 / ratio_start
     for iteration in range(ITERS):
-        partial_image = lax.dot_general(
-            full, design, (((1,), (1,)), ((), ())), preferred_element_type=jnp.float32
-        )
-        image = coef_sum(partial_image, coef_count, 3 + iteration)
-        partial = jnp.dot(image, design, preferred_element_type=jnp.float32)
         factor_next = 1.0 / (2.0 * ratio_start - factor)
-        last = iteration == ITERS - 1
-        state, full = exchange(
-            2 if last else 1, partial, state, factor_next * factor, 2.0 * factor_next / HALF_WIDTH
-        )
+        keep.append(factor_next * factor)
+        gain.append(2.0 * factor_next / HALF_WIDTH)
         factor = factor_next
+    keep = jnp.stack(keep)[:, :, None]
+    gain = jnp.stack(gain)[:, :, None]
+    if direct:
+        full = solve(
+            obs_count, coef_count, observations, design, shifts[:, None], keep, gain
+        )
+    else:
+        full = solve_plain(coef_count, observations, design, shifts[:, None], keep, gain)
     block_count = coef_count * BPO
     block_rows = NL // block_count
     owned_rows = kdev // NL

time: 171 us -> 113 us (0.66)
  matrix products: 56 us -> 2.81 us
  Pallas kernels: 100 us -> 97.9 us
    dot_general x5 -> x0, matrix products: 53.2 us -> none  [the longest x2 24.3 us: body(): lax.dot_general(full, design, (((1,), (1,)), ((), ())), preferred_element...]
    pallas_call x5 -> x1, Pallas kernels: 66.5 us -> 63.4 us  [solve(): pl.pallas_call(functools.partial(solver_kernel, n, nc), out_shape=jax.Sha...]
where the time goes in v2:
time: 113 us
  Pallas kernels  97.9 us (87%)
  local copies, waits for them, and re-layouts  8.91 us (8%)
  matrix products  2.81 us (2%)
  other arithmetic  2.44 us (2%)
    pallas_call x1, Pallas kernels, solve(): pl.pallas_call(functools.partial(solver_kernel, n, nc), out_shape=jax.Sha...  63.4 us
    pallas_call x2, Pallas kernels, coef_scatter(): pl.pallas_call(functools.partial(scatter_kernel, n), out_shape=jax.ShapeD...  19 us
    pallas_call x1, Pallas kernels, place(): pl.pallas_call(functools.partial(place_kernel, width), out_shape=jax.Shap...  10.8 us
    pallas_call x1, Pallas kernels, legendre(): pl.pallas_call(legendre_kernel, out_shape=jax.ShapeDtypeStruct((2, lats,...  4.63 us
    unnamed x8, local copies, waits for them, and re-layouts  2.86 us

profile of v2, /device:TPU:0, one launch (start us, length us, event | category | flops | bytes accessed | tf_op | source)
XLA Modules:
  0.0 112.8 jit_solution(9949938946427067190)
XLA Ops:
  0.6 0.0 copy-start.1
  0.6 0.0 copy-start.2
  0.7 0.9 select_reduce_fusion.1
  1.6 0.1 copy.25.keep_ref
  1.7 0.1 copy.26.gain_ref
  1.7 0.1 copy.24.shift_ref
  1.8 0.0 copy-start
  1.8 0.7 copy-done
  2.6 63.4 %solve.1.sol_ref = bf16[8,9216]{1,0:T(8,128)(2,1)S(1)} custom-call(bf16[8,1024]{1,0:T(8,128)(2,1)S(1)} %copy-done, bf16[1024,9216]{1,0:T(8,128)(2,1)} %design_ref.1, f32[8,1]{1,0:T(8,128)S(1)} %copy.24.shift_ref, f32[3,8,1]{2,1,0:T(8,128)S(1)} %copy.25.keep_ref, f32[3,8,1]{2,1,0:T(8,128)S(1)} %copy.26.gain_ref), custom_call_target="tpu_custom_call" | custom-call | tf_op jit(solution)/shard_map/solve/pallas_call | solution.py:160
  66.0 0.0 copy-done.1
  66.0 0.1 add_select_fusion.4
  66.1 0.0 copy-done.2
  66.1 0.1 select_reduce_fusion.2
  66.2 0.2 select_reduce_fusion
  66.3 0.1 add_select_fusion.2
  66.4 10.8 %place.1 = f32[1536,192]{1,0:T(8,128)S(1)} custom-call(s32[1,9216]{1,0:T(1,128)S(1)} %bitcast.44, s32[1,9216]{1,0:T(1,128)S(1)} %bitcast.43, bf16[8,9216]{1,0:T(8,128)(2,1)S(1)} %solve.1.sol_ref), custom_call_target="tpu_custom_call" | custom-call | tf_op jit(solution)/shard_map/place/pallas_call | solution.py:287
  77.3 1.0 convert_element_type.33
  78.2 13.1 %coef_scatter.2 = f32[384,192]{1,0:T(8,128)} custom-call(bf16[4,384,192]{2,1,0:T(8,128)(2,1)} %bitcast.45), custom_call_target="tpu_custom_call" | custom-call | tf_op jit(solution)/shard_map/coef_scatter/pallas_call | solution.py:249
  91.3 1.9 %copy.27 = f32[384,192]{0,1:T(8,128)} copy(f32[384,192]{1,0:T(8,128)} %coef_scatter.2) | data formatting | bytes 589824 | tf_op jit(solution)/shard_map/coef_scatter/pallas_call | solution.py:249
  93.2 0.1 dynamic-slice_multiply_fusion
  93.3 0.1 iota_add_fusion
  93.3 0.1 add.126
  93.4 0.1 broadcast_in_dim.71
  93.5 0.1 convert_element_type.31
  93.6 0.6 add.127.order_ref
  94.2 0.7 add.131.cos_ref
  94.9 0.7 add.132.sin_ref
  95.6 4.6 %legendre.1 = f32[2,4,384]{2,1,0:T(4,128)} custom-call(f32[4,384]{1,0:T(4,128)} %add.127.order_ref, f32[4,384]{1,0:T(4,128)} %add.131.cos_ref, f32[4,384]{1,0:T(4,128)} %add.132.sin_ref, f32[192,384]{1,0:T(8,128)} %bitcast.46), custom_call_target="tpu_custom_call" | custom-call | tf_op jit(solution)/shard_map/legendre/pallas_call | solution.py:367
  100.2 0.7 fusion.53
  100.9 0.1 squeeze.6
  101.0 1.1 fusion.6
  102.1 0.1 squeeze.7
  102.2 1.7 %fusion.x_ref = f32[4,8,1024]{2,1,0:T(8,128)} fusion(f32[4,8,1024]{2,1,0:T(8,128)S(1)} %fusion.6, f32[4,48,8]{2,1,0:T(8,128)S(1)} %squeeze.7, s32[48]{0:T(128)S(1)} %get-tuple-element.12), kind=kOutput, calls=%fused_computation.1 | convolution fusion | flops 19628032 | bytes 268480 | tf_op jit(solution)/shard_map/lqc,qk->lck/dot_general | solution.py:453
  104.0 5.9 %coef_scatter.3 = f32[8,1024]{1,0:T(8,128)} custom-call(f32[4,8,1024]{2,1,0:T(8,128)} %fusion.x_ref), custom_call_target="tpu_custom_call" | custom-call | tf_op jit(solution)/shard_map/coef_scatter/pallas_call | solution.py:249
  109.9 1.4 %copy.31 = f32[8,1,1024]{2,1,0:T(1,128)} copy(f32[8,1,1024]{2,0,1:T(8,128)} %bitcast.48) | data formatting | bytes 65536
  111.3 0.8 reshape.122
  112.1 0.7 copy.30
  (5 shorter events, 0.1 us)
Async XLA Ops:
  0.6 65.4 %copy-start.1 = (s32[9216]{0:T(1024)S(1)}, s32[9216]{0:T(1024)}, u32[]{:S(2)}) copy-start(s32[9216]{0:T(1024)} %param.10) | copy-start | bytes 110596
  0.6 65.4 %copy-start.2 = (s32[8]{0:T(128)S(1)}, s32[8]{0:T(128)}, u32[]{:S(2)}) copy-start(s32[8]{0:T(128)} %param.11) | copy-start | bytes 100
  1.8 0.7 copy-start

commit v3 on v2

--- a/solution.py
+++ b/solution.py
@@ -295,6 +295,99 @@
     )(rows, cols, sol)
 
 
+def share_kernel(
+    n, nc, width, row_ref, col_ref, sol_ref, out_ref,
+    spread, acc, sent, landed, gathered, send_a, recv_a, send_b, recv_b,
+):
+    me = lax.axis_index("obs")
+    mine = lax.axis_index("coef")
+    owned = NL // nc
+    sub = owned // n
+    span = sub * COLS
+    barrier = pltpu.get_barrier_semaphore()
+    for axis, count, rank in (("obs", n, me), ("coef", nc, mine)):
+        for step in range(1, count):
+            pl.semaphore_signal(
+                barrier,
+                inc=1,
+                device_id={axis: lax.rem(rank + step, count)},
+                device_id_type=MESH,
+            )
+    acc[...] = jnp.zeros_like(acc)
+    wide = jnp.zeros((COLS, width), jnp.int32)
+
+    def step_of(index, carry):
+        at = pl.ds(pl.multiple_of(index * width, 128), width)
+        values = sol_ref[:, at].astype(jnp.float32)
+        rows = row_ref[:, at] + wide - me * sub
+        for pair in range(nc * sub // 2):
+            halves = []
+            for entry in (2 * pair, 2 * pair + 1):
+                row = entry // sub * owned + entry % sub
+                halves.append(jnp.where(rows == row, values, 0.0))
+            both = jnp.concatenate(halves, axis=0)
+            spread[pair * 2 * COLS : (pair + 1) * 2 * COLS, :] = both.astype(jnp.bfloat16)
+        degree = lax.broadcasted_iota(jnp.int32, (NL, width), 0)
+        hot = jnp.where(degree == col_ref[:, at], 1.0, 0.0).astype(jnp.bfloat16)
+        acc[...] += lax.dot_general(
+            spread[...], hot, (((1,), (1,)), ((), ())), preferred_element_type=jnp.float32
+        )
+        return carry
+
+    lax.fori_loop(0, sol_ref.shape[1] // width, step_of, 0)
+    for owner in range(nc):
+        sent[owner] = acc[owner * span : (owner + 1) * span, :].astype(jnp.bfloat16)
+    pl.semaphore_wait(barrier, n + nc - 2)
+    copies = []
+    for step in range(1, nc):
+        target = lax.rem(mine + step, nc)
+        copy = push("coef", nc, mine, step, sent.at[target], landed.at[step], send_a, recv_a)
+        copy.start()
+        copies.append(copy)
+    total = sent[mine].astype(jnp.float32)
+    for step in range(1, nc):
+        copies[step - 1].wait()
+        total = total + landed[step].astype(jnp.float32)
+    gathered[0] = total.astype(jnp.bfloat16)
+    copies = []
+    for step in range(1, n):
+        copy = push("obs", n, me, step, gathered.at[0], gathered.at[step], send_b, recv_b)
+        copy.start()
+        copies.append(copy)
+    for step in range(n):
+        if step:
+            copies[step - 1].wait()
+        origin = lax.rem(me + n - step, n)
+        at = pl.ds(pl.multiple_of(origin * span, COLS), span)
+        out_ref[at, :] = gathered[step].astype(jnp.float32)
+
+
+def share(n, nc, rows, cols, sol):
+    kdev = sol.shape[1]
+    width = next(w for w in (1152, 512, 384, 256, 128) if kdev % w == 0)
+    part = NL // n * COLS
+    span = part // nc
+    return pl.pallas_call(
+        functools.partial(share_kernel, n, nc, width),
+        out_shape=jax.ShapeDtypeStruct((n * span, NL), jnp.float32),
+        in_specs=[VMEM_SPEC] * 3,
+        out_specs=VMEM_SPEC,
+        scratch_shapes=[
+            pltpu.VMEM((part, width), jnp.bfloat16),
+            pltpu.VMEM((part, NL), jnp.float32),
+            pltpu.VMEM((nc, span, NL), jnp.bfloat16),
+            pltpu.VMEM((nc, span, NL), jnp.bfloat16),
+            pltpu.VMEM((n, span, NL), jnp.bfloat16),
+        ]
+        + [pltpu.SemaphoreType.DMA((nc,))] * 2
+        + [pltpu.SemaphoreType.DMA((n,))] * 2,
+        compiler_params=pltpu.CompilerParams(
+            collective_id=1, has_side_effects=True, vmem_limit_bytes=32 << 20
+        ),
+        name="share",
+    )(rows, cols, sol)
+
+
 def table_of(level, order, valid):
     product = (level - order) * (level + order)
     denom = jnp.where(valid, product, 1.0)
@@ -306,8 +399,11 @@
     return jnp.where(valid, first, 0.0), jnp.where(valid, second, 0.0)
 
 
-def legendre_kernel(order_ref, cos_ref, sin_ref, w_ref, out_ref, a_c, b_c, a_s, b_s, grow):
+def legendre_kernel(
+    order_ref, cos_ref, sin_ref, local_ref, out_ref, a_c, b_c, a_s, b_s, grow, w_ref
+):
     lats, lanes = cos_ref.shape
+    w_ref[...] = local_ref[...].T
     order = order_ref[0:1, :]
     other = float(NL) - order
     count = lax.broadcasted_iota(jnp.int32, (NL, lanes), 0).astype(jnp.float32)
@@ -360,7 +456,7 @@
 
 
 def legendre(orders, colatitude, w):
-    lanes = w.shape[1]
+    lanes = w.shape[0]
     lats = colatitude.shape[0]
     spread = jnp.zeros((lats, lanes), jnp.float32)
     table = pltpu.VMEM((NL, lanes), jnp.float32)
@@ -369,7 +465,7 @@
         out_shape=jax.ShapeDtypeStruct((2, lats, lanes), jnp.float32),
         in_specs=[VMEM_SPEC] * 4,
         out_specs=VMEM_SPEC,
-        scratch_shapes=[table] * 5,
+        scratch_shapes=[table] * 6,
         name="legendre",
     )(
         orders[None, :] + spread,
@@ -434,10 +530,13 @@
         axis=0,
     )
     owner_row = place_of * block_rows + paired_row % block_rows
-    placed = place(owner_row[None, :], column[None, :], full)
     lanes = owned_rows * COLS
-    outgoing = placed.astype(jnp.bfloat16).reshape(coef_count, lanes, NL)
-    local = coef_scatter(outgoing, coef_count, 5).T
+    if direct and owned_rows % (2 * obs_count) == 0:
+        local = share(obs_count, coef_count, owner_row[None, :], column[None, :], full)
+    else:
+        placed = place(owner_row[None, :], column[None, :], full)
+        outgoing = placed.astype(jnp.bfloat16).reshape(coef_count, lanes, NL)
+        local = coef_scatter(outgoing, coef_count, 5)
     my_blocks = lax.dynamic_slice_in_dim(order_map, coef_rank * BPO, BPO)
     row_offsets = jnp.arange(block_rows, dtype=jnp.int32)
     owned_canon = (my_blocks[:, None] * block_rows + row_offsets[None, :]).reshape(owned_rows)

time: 113 us -> 100 us (0.88)
  Pallas kernels: 97.9 us -> 87.2 us
    pallas_call x2 -> x1, Pallas kernels: 19 us -> 5.63 us  [coef_scatter(): pl.pallas_call(functools.partial(scatter_kernel, n), out_shape=jax.ShapeD...]
    pallas_call x1, Pallas kernels: 10.8 us -> 13.2 us  [share(): pl.pallas_call(functools.partial(share_kernel, n, nc, width), out_shape=j...]
    pallas_call x1 -> x0, local copies, waits for them, and re-layouts: 1.85 us -> none  [coef_scatter(): pl.pallas_call(functools.partial(scatter_kernel, n), out_shape=jax.ShapeD...]
    unnamed x8 -> x10, local copies, waits for them, and re-layouts: 2.86 us -> 3.59 us
where the time goes in v3:
time: 100 us
  Pallas kernels  87.2 us (87%)
  local copies, waits for them, and re-layouts  7.8 us (8%)
  matrix products  2.79 us (3%)
  other arithmetic  1.48 us (1%)
    pallas_call x1, Pallas kernels, solve(): pl.pallas_call(functools.partial(solver_kernel, n, nc), out_shape=jax.Sha...  63.4 us
    pallas_call x1, Pallas kernels, share(): pl.pallas_call(functools.partial(share_kernel, n, nc, width), out_shape=j...  13.2 us
    pallas_call x1, Pallas kernels, coef_scatter(): pl.pallas_call(functools.partial(scatter_kernel, n), out_shape=jax.ShapeD...  5.63 us
    pallas_call x1, Pallas kernels, legendre(): pl.pallas_call(legendre_kernel, out_shape=jax.ShapeDtypeStruct((2, lats,...  4.92 us
    unnamed x10, local copies, waits for them, and re-layouts  3.59 us

profile of v3, /device:TPU:0, one launch (start us, length us, event | category | flops | bytes accessed | tf_op | source)
XLA Modules:
  0.0 100.0 jit_solution(7040279081586045743)
XLA Ops:
  0.6 0.0 copy-start.2
  0.6 0.0 copy-start.3
  0.7 0.9 select_reduce_fusion.1
  1.6 0.1 copy.23.keep_ref
  1.7 0.1 copy.24.gain_ref
  1.7 0.1 copy.22.shift_ref
  1.8 0.0 copy-start.1
  1.8 0.7 copy-done.1
  2.6 63.4 %solve.1.sol_ref = bf16[8,9216]{1,0:T(8,128)(2,1)S(1)} custom-call(bf16[8,1024]{1,0:T(8,128)(2,1)S(1)} %copy-done.1, bf16[1024,9216]{1,0:T(8,128)(2,1)} %design_ref.1, f32[8,1]{1,0:T(8,128)S(1)} %copy.22.shift_ref, f32[3,8,1]{2,1,0:T(8,128)S(1)} %copy.23.keep_ref, f32[3,8,1]{2,1,0:T(8,128)S(1)} %copy.24.gain_ref), custom_call_target="tpu_custom_call" | custom-call | tf_op jit(solution)/shard_map/solve/pallas_call | solution.py:160
  66.0 0.0 copy-done.2
  66.0 0.1 add_select_fusion.4
  66.1 0.0 copy-done.3
  66.1 0.1 select_reduce_fusion.2
  66.2 0.2 select_reduce_fusion
  66.3 0.1 add_select_fusion.2
  66.4 13.2 %share.1.local_ref = f32[384,192]{1,0:T(8,128)S(1)} custom-call(s32[1,9216]{1,0:T(1,128)S(1)} %bitcast.42, s32[1,9216]{1,0:T(1,128)S(1)} %bitcast.41, bf16[8,9216]{1,0:T(8,128)(2,1)S(1)} %solve.1.sol_ref), custom_call_target="tpu_custom_call" | custom-call | tf_op jit(solution)/shard_map/share/pallas_call | solution.py:370
  79.6 0.0 copy-start
  79.6 0.7 copy-done
  80.3 0.1 dynamic-slice_multiply_fusion
  80.4 0.1 iota_add_fusion
  80.5 0.1 add.126
  80.6 0.1 broadcast_in_dim.71
  80.7 0.1 convert_element_type.28
  80.8 0.6 add.127.order_ref
  81.4 0.7 add.131.cos_ref
  82.1 0.7 add.132.sin_ref
  82.7 4.9 %legendre.1 = f32[2,4,384]{2,1,0:T(4,128)} custom-call(f32[4,384]{1,0:T(4,128)} %add.127.order_ref, f32[4,384]{1,0:T(4,128)} %add.131.cos_ref, f32[4,384]{1,0:T(4,128)} %add.132.sin_ref, f32[384,192]{1,0:T(8,128)} %copy-done), custom_call_target="tpu_custom_call" | custom-call | tf_op jit(solution)/shard_map/legendre/pallas_call | solution.py:463
  87.7 0.7 fusion.53
  88.4 0.1 squeeze.6
  88.5 1.1 %fusion.6 = f32[4,8,1024]{2,1,0:T(8,128)S(1)} fusion(f32[4,48,8]{2,1,0:T(8,128)S(1)} %squeeze.6, s32[48]{0:T(128)S(1)} %add.126), kind=kOutput, calls=%fused_computation.15 | convolution fusion | flops 19562496 | bytes 137408 | tf_op jit(solution)/shard_map/lqc,qk->lck/dot_general | solution.py:551
  89.6 0.1 squeeze.7
  89.7 1.7 %fusion.x_ref = f32[4,8,1024]{2,1,0:T(8,128)} fusion(f32[4,8,1024]{2,1,0:T(8,128)S(1)} %fusion.6, f32[4,48,8]{2,1,0:T(8,128)S(1)} %squeeze.7, s32[48]{0:T(128)S(1)} %get-tuple-element.12), kind=kOutput, calls=%fused_computation.1 | convolution fusion | flops 19628032 | bytes 268480 | tf_op jit(solution)/shard_map/lqc,qk->lck/dot_general | solution.py:552
  91.4 5.6 %coef_scatter.1 = f32[8,1024]{1,0:T(8,128)} custom-call(f32[4,8,1024]{2,1,0:T(8,128)} %fusion.x_ref), custom_call_target="tpu_custom_call" | custom-call | tf_op jit(solution)/shard_map/coef_scatter/pallas_call | solution.py:249
  97.0 1.4 %copy.28 = f32[8,1,1024]{2,1,0:T(1,128)} copy(f32[8,1,1024]{2,0,1:T(8,128)} %bitcast.44) | data formatting | bytes 65536
  98.4 0.8 reshape.118
  99.3 0.7 copy.27
  (5 shorter events, 0.1 us)
Async XLA Ops:
  0.6 65.4 %copy-start.2 = (s32[9216]{0:T(1024)S(1)}, s32[9216]{0:T(1024)}, u32[]{:S(2)}) copy-start(s32[9216]{0:T(1024)} %param.10) | copy-start | bytes 110596
  0.6 65.4 %copy-start.3 = (s32[8]{0:T(128)S(1)}, s32[8]{0:T(128)}, u32[]{:S(2)}) copy-start(s32[8]{0:T(128)} %param.11) | copy-start | bytes 100
  1.8 0.7 copy-start.1
  79.6 0.7 copy-start

commit v4 on v3

--- a/solution.py
+++ b/solution.py
@@ -97,7 +97,7 @@
             scatter_copy(rnd, step).start()
             return carry
 
-        lax.fori_loop(1, n, compute, 0)
+        lax.fori_loop(1, n, compute, 0, unroll=True)
         if rnd == 0:
             load(0).wait()
         total = jnp.dot(left, held[0], preferred_element_type=jnp.float32)
@@ -127,7 +127,7 @@
             )
             return carry
 
-        lax.fori_loop(0, n, compute, 0)
+        lax.fori_loop(0, n, compute, 0, unroll=True)
         for step in range(1, nc):
             image_copy(rnd, step).start()
         image = image_sent[...]
@@ -400,11 +400,11 @@
 
 
 def legendre_kernel(
-    order_ref, cos_ref, sin_ref, local_ref, out_ref, a_c, b_c, a_s, b_s, grow, w_ref
+    angle_ref, local_ref, out_ref, a_c, b_c, a_s, b_s, grow, w_ref
 ):
-    lats, lanes = cos_ref.shape
+    lats, lanes = angle_ref.shape[1:]
     w_ref[...] = local_ref[...].T
-    order = order_ref[0:1, :]
+    order = angle_ref[0, 0:1, :]
     other = float(NL) - order
     count = lax.broadcasted_iota(jnp.int32, (NL, lanes), 0).astype(jnp.float32)
     wide = jnp.zeros((NL, lanes), jnp.float32)
@@ -421,10 +421,10 @@
     grow[...] = jnp.where(
         count == 1.0, math.sqrt(3.0), jnp.sqrt((2.0 * safe + 1.0) / (2.0 * safe))
     )
-    cosine = cos_ref[...]
-    sine = sin_ref[...]
+    cosine = angle_ref[1]
+    sine = angle_ref[2]
     zero = cosine * 0.0
-    low = order_ref[...]
+    low = angle_ref[0]
     high = float(NL) - low
 
     def climb(degree, carry):
@@ -458,19 +458,22 @@
 def legendre(orders, colatitude, w):
     lanes = w.shape[0]
     lats = colatitude.shape[0]
-    spread = jnp.zeros((lats, lanes), jnp.float32)
+    which = lax.broadcasted_iota(jnp.int32, (3, lats, lanes), 0)
+    angles = jnp.where(
+        which == 0,
+        orders[None, None, :],
+        jnp.where(which == 1, jnp.cos(colatitude)[:, None], jnp.sin(colatitude)[:, None]),
+    )
     table = pltpu.VMEM((NL, lanes), jnp.float32)
     return pl.pallas_call(
         legendre_kernel,
         out_shape=jax.ShapeDtypeStruct((2, lats, lanes), jnp.float32),
-        in_specs=[VMEM_SPEC] * 4,
+        in_specs=[VMEM_SPEC] * 2,
         out_specs=VMEM_SPEC,
         scratch_shapes=[table] * 6,
         name="legendre",
     )(
-        orders[None, :] + spread,
-        jnp.cos(colatitude)[:, None] + spread,
-        jnp.sin(colatitude)[:, None] + spread,
+        angles,
         w,
     )
 

time: 100 us -> 98.4 us (0.984)
  local copies, waits for them, and re-layouts: 7.8 us -> 5.87 us
    add x3 -> x0, local copies, waits for them, and re-layouts: 1.94 us -> none  [the longest x1 0.68 us: legendre(): jnp.cos(colatitude)[:, None] + spread]
where the time goes in v4:
time: 98.4 us; the launch traced here: 97.9 us
  Pallas kernels  86.3 us (88%)
  local copies, waits for them, and re-layouts  5.87 us (6%)
  matrix products  2.8 us (3%)
  other arithmetic  2.17 us (2%)
    pallas_call x1, Pallas kernels, solve(): pl.pallas_call(functools.partial(solver_kernel, n, nc), out_shape=jax.Sha...  63.1 us
    pallas_call x1, Pallas kernels, share(): pl.pallas_call(functools.partial(share_kernel, n, nc, width), out_shape=j...  12.7 us
    pallas_call x1, Pallas kernels, coef_scatter(): pl.pallas_call(functools.partial(scatter_kernel, n), out_shape=jax.ShapeD...  5.64 us
    pallas_call x1, Pallas kernels, legendre(): pl.pallas_call(legendre_kernel, out_shape=jax.ShapeDtypeStruct((2, lats,...  4.89 us
    unnamed x10, local copies, waits for them, and re-layouts  3.61 us

profile of v4, /device:TPU:0, one launch (start us, length us, event | category | flops | bytes accessed | tf_op | source)
XLA Modules:
  0.0 97.9 jit_solution(4867024602785663848)
XLA Ops:
  0.6 0.0 copy-start.2
  0.6 0.0 copy-start.3
  0.7 0.9 select_reduce_fusion.1
  1.6 0.1 copy.23.keep_ref
  1.7 0.1 copy.24.gain_ref
  1.7 0.1 copy.22.shift_ref
  1.8 0.0 copy-start.1
  1.8 0.7 copy-done.1
  2.6 63.1 %solve.1.sol_ref = bf16[8,9216]{1,0:T(8,128)(2,1)S(1)} custom-call(bf16[8,1024]{1,0:T(8,128)(2,1)S(1)} %copy-done.1, bf16[1024,9216]{1,0:T(8,128)(2,1)} %design_ref.1, f32[8,1]{1,0:T(8,128)S(1)} %copy.22.shift_ref, f32[3,8,1]{2,1,0:T(8,128)S(1)} %copy.23.keep_ref, f32[3,8,1]{2,1,0:T(8,128)S(1)} %copy.24.gain_ref), custom_call_target="tpu_custom_call" | custom-call | tf_op jit(solution)/shard_map/solve/pallas_call | solution.py:160
  65.7 0.0 copy-done.2
  65.7 0.1 add_select_fusion.4
  65.7 0.0 copy-done.3
  65.8 0.1 select_reduce_fusion.2
  65.8 0.2 select_reduce_fusion
  66.0 0.1 add_select_fusion.2
  66.1 12.7 %share.1.local_ref = f32[384,192]{1,0:T(8,128)S(1)} custom-call(s32[1,9216]{1,0:T(1,128)S(1)} %bitcast.42, s32[1,9216]{1,0:T(1,128)S(1)} %bitcast.41, bf16[8,9216]{1,0:T(8,128)(2,1)S(1)} %solve.1.sol_ref), custom_call_target="tpu_custom_call" | custom-call | tf_op jit(solution)/shard_map/share/pallas_call | solution.py:370
  78.8 0.0 copy-start
  78.8 0.7 copy-done
  79.5 0.1 dynamic-slice_multiply_fusion
  79.6 0.1 iota_add_fusion
  79.7 0.1 add.97
  79.8 0.1 broadcast_in_dim.95
  79.8 0.1 convert_element_type.21
  80.0 0.7 select_select_fusion.angle_ref
  80.7 4.9 %legendre.1 = f32[2,4,384]{2,1,0:T(4,128)} custom-call(f32[3,4,384]{2,1,0:T(4,128)} %select_select_fusion.angle_ref, f32[384,192]{1,0:T(8,128)} %copy-done), custom_call_target="tpu_custom_call" | custom-call | tf_op jit(solution)/shard_map/legendre/pallas_call | solution.py:468
  85.6 0.7 fusion.53
  86.3 0.1 squeeze.6
  86.4 1.1 %fusion.6 = f32[4,8,1024]{2,1,0:T(8,128)S(1)} fusion(f32[4,48,8]{2,1,0:T(8,128)S(1)} %squeeze.6, s32[48]{0:T(128)S(1)} %add.97), kind=kOutput, calls=%fused_computation.15 | convolution fusion | flops 19562496 | bytes 137408 | tf_op jit(solution)/shard_map/lqc,qk->lck/dot_general | solution.py:554
  87.5 0.1 squeeze.7
  87.6 1.7 %fusion.x_ref = f32[4,8,1024]{2,1,0:T(8,128)} fusion(f32[4,8,1024]{2,1,0:T(8,128)S(1)} %fusion.6, f32[4,48,8]{2,1,0:T(8,128)S(1)} %squeeze.7, s32[48]{0:T(128)S(1)} %get-tuple-element.12), kind=kOutput, calls=%fused_computation.1 | convolution fusion | flops 19628032 | bytes 268480 | tf_op jit(solution)/shard_map/lqc,qk->lck/dot_general | solution.py:555
  89.3 5.6 %coef_scatter.1 = f32[8,1024]{1,0:T(8,128)} custom-call(f32[4,8,1024]{2,1,0:T(8,128)} %fusion.x_ref), custom_call_target="tpu_custom_call" | custom-call | tf_op jit(solution)/shard_map/coef_scatter/pallas_call | solution.py:249
  94.9 1.4 %copy.28 = f32[8,1,1024]{2,1,0:T(1,128)} copy(f32[8,1,1024]{2,0,1:T(8,128)} %bitcast.44) | data formatting | bytes 65536
  96.4 0.8 reshape.107
  97.2 0.7 copy.27
  (6 shorter events, 0.1 us)
Async XLA Ops:
  0.6 65.0 %copy-start.2 = (s32[9216]{0:T(1024)S(1)}, s32[9216]{0:T(1024)}, u32[]{:S(2)}) copy-start(s32[9216]{0:T(1024)} %param.10) | copy-start | bytes 110596
  0.6 65.1 %copy-start.3 = (s32[8]{0:T(128)S(1)}, s32[8]{0:T(128)}, u32[]{:S(2)}) copy-start(s32[8]{0:T(128)} %param.11) | copy-start | bytes 100
  1.8 0.7 copy-start.1
  78.8 0.8 copy-start
